TPU v7x, 256 devices: a whole 4x4x8 slice. The times are simulated.
256 devices in a mesh: sect: 2 (over core), gy: 16 (over x, y), gx: 8 (over z).
Axes of the slice: x: 4, y: 4, z: 8, core: 2. Of those that a mesh axis runs over, the one named last changes fastest.
Arguments:
- adjoint_init: float32 [2, 32, 512, 2048], P('sect', None, 'gy', 'gx'), may hold values from -6 to 6
- diffusivity: float32 [2, 512, 2048], P('sect', 'gy', 'gx'), may hold values from 0.02 to 0.12
- mixing: float32 [2, 32, 32], P('sect'), may hold values from -0.75 to 0.75
- coupling: float32 [2, 32, 8], P('sect'), may hold values from -6 to 6
- history: float32 [2, 4, 4, 512, 2048], P('sect', None, None, 'gy', 'gx'), may hold values from -6 to 6
- extract: float32 [4, 32], replicated, may hold values from -3 to 3
- land_mask: int32 [512, 2048], P('gy', 'gx'), may hold values 0 or 1
- regrid: float32 [128, 128, 128], P(('gy', 'gx')), may hold values from -0.5 to 0.5
- atmos_tile_index: int32 [16384, 1], replicated, may hold values from 0 to 127; in each aligned block of 128 rows (0 to 127, 128 to 255, ...) at most 2 rows name the same one
- ocean_block_index: int32 [16384], replicated, may hold values from 0 to 63
- atmos_block_index: int32 [16384], replicated, may hold values from 0 to 63
Outputs:
- adjoint_state: float32 [2, 32, 512, 2048], P('sect', None, 'gy', 'gx')
Inputs may be any that keep to these rules, and one draw needn't show every extreme that they name: `atmos_tile_index`: list rows i*128 to (i+1)*128 - 1 are ocean tile i's entries; among them at most 2 name the same atmosphere tile, and exactly 2 do so for some atmosphere tile.
All inputs are finite; a program needn't handle non-finite values. No bound on the sum of `land_mask` on one device may be relied on, other than what follows from the above.
Results may differ from a plain program's by a relative error of at most 0.0001.
Values sent between devices are 32-bit elements; how exact they have to be, the bound alone decides.
A program may use at most 64 MiB of HBM per device.

v0:
```python
import functools

import jax
import jax.numpy as jnp
from jax import lax
from jax.experimental import pallas as pl
from jax.experimental.pallas import tpu as pltpu
from jax.sharding import PartitionSpec as P

MESH = pl.DeviceIdType.MESH
F32, BF16 = jnp.float32, jnp.bfloat16
NC, NY, NX = 32, 32, 256
STEPS, FIELDS = 4, 4
SUB = 8
BANDS = NY // SUB
CELLS = 128
BLOCKS = NY * NX // CELLS
CAP = 2
NT = (((1,), (1,)), ((), ()))


def iota(shape, axis):
    return lax.broadcasted_iota(jnp.int32, shape, axis)


def split(x):
    hi = x.astype(BF16)
    return hi, (x - hi.astype(F32)).astype(BF16)


def mm(a, b):
    return jnp.dot(a, b, preferred_element_type=F32)


def mm_nt(a, b):
    return lax.dot_general(a, b, NT, preferred_element_type=F32)


def onehot(cond):
    return jnp.where(cond, 1.0, 0.0).astype(BF16)


def widen(small):
    rows, columns = small.shape
    left = onehot(iota((rows * SUB, rows), 0) // SUB == iota((rows * SUB, rows), 1))
    right = onehot(iota((columns, columns * SUB), 1) // SUB == iota((columns, columns * SUB), 0))
    big = (rows * SUB, columns * SUB)
    same = iota(big, 0) % SUB == iota(big, 1) % SUB
    return [
        jnp.where(same, mm(mm(left, part).astype(BF16), right), 0.0).astype(BF16)
        for part in split(small)
    ]


def block_place(block):
    return (block % 2) * NY + block // 2


def kernel(
    n_gy, n_gx,
    adj_hbm, dif_hbm, mix_hbm, cou_hbm, his_hbm, ext_hbm, msk_hbm, reg_hbm, dst_hbm, src_hbm, blk_hbm,
    out_hbm,
    mix_ref, cou_ref, ext_ref, reg_ref, dst_ref, src_ref, blk_ref,
    state, wet, dif, hist, far, vee, acc, u_hi, u_lo, k_hi, k_lo, c_own, c_far, e_hi, e_lo, r_hi, r_lo,
    pick, place, packed, arrived, row_out, row_in, col_out, col_in,
    load_sem, far_send, far_recv, halo_send, halo_recv, a2a_send, a2a_recv, out_sem,
):
    sect, gy, gx = lax.axis_index("sect"), lax.axis_index("gy"), lax.axis_index("gx")
    tiles = n_gy * n_gx
    me = gy * n_gx + gx
    is_ocean, is_atmos = sect == 0, sect == 1
    west, east = lax.rem(gx + n_gx - 1, n_gx), lax.rem(gx + 1, n_gx)
    has_north, has_south = gy > 0, gy < n_gy - 1
    barrier = pltpu.get_barrier_semaphore()

    loads = [
        pltpu.make_async_copy(source, target, load_sem.at[j])
        for j, (source, target) in enumerate(
            (
                (mix_hbm.at[0], mix_ref), (cou_hbm.at[0], cou_ref), (ext_hbm, ext_ref), (dst_hbm, dst_ref),
                (src_hbm, src_ref), (blk_hbm, blk_ref), (reg_hbm.at[0], reg_ref), (dif_hbm.at[0], dif),
                (msk_hbm, wet), (adj_hbm.at[0], state), (his_hbm.at[0], hist),
            )
        )
    ]
    for load in loads:
        load.start()

    def signal(s, y, x):
        pl.semaphore_signal(barrier, inc=1, device_id=(s, y, x), device_id_type=MESH)

    @pl.when(gy == 0)
    def _():
        row_in[:, 0] = jnp.zeros_like(row_in[:, 0])

    @pl.when(gy == n_gy - 1)
    def _():
        row_in[:, 1] = jnp.zeros_like(row_in[:, 1])

    signal(sect, gy, west)
    signal(sect, gy, east)

    @pl.when(has_north)
    def _():
        signal(sect, gy - 1, gx)

    @pl.when(has_south)
    def _():
        signal(sect, gy + 1, gx)

    @pl.when(is_ocean)
    def _():
        signal(1, gy, gx)

    @pl.when(is_atmos)
    def _():
        def one(t, carry):
            signal(0, lax.rem(gy + t // n_gx, n_gy), lax.rem(gx + t % n_gx, n_gx))
            return carry

        lax.fori_loop(0, tiles, one, 0)

    for load in loads[:-1]:
        load.wait()

    k_hi[...], k_lo[...] = widen(mix_ref[...].T)
    for column, ref in ((0, c_own), (FIELDS, c_far)):
        hi, lo = widen(cou_ref[column : column + FIELDS, :].T)
        ref[...] = jnp.concatenate([hi, hi, lo], axis=1)

    @pl.when(is_ocean)
    def _():
        e_hi[...], e_lo[...] = widen(ext_ref[...])
        r_hi[...], r_lo[...] = split(reg_ref[...])
        entries = dst_ref.shape[1]
        dest = dst_ref[pl.ds(me, 1), :]
        source = block_place(src_ref[pl.ds(me, 1), :])
        dest_row = jnp.broadcast_to(dest, (entries, entries))
        dest_col = dest_row.T
        square = (entries, entries)
        earlier = (dest_row == dest_col) & (iota(square, 0) < iota(square, 1))
        rank = jnp.sum(jnp.where(earlier, 1, 0), axis=0, keepdims=True)
        position = dest * CAP + rank
        slots = tiles * CAP * FIELDS
        goes = onehot(jnp.broadcast_to(position, (slots, entries)) == iota((slots, entries), 0) // FIELDS)
        wide = FIELDS * BLOCKS
        reads = onehot(jnp.broadcast_to(source, (wide, entries)) == iota((wide, entries), 0) % BLOCKS)
        field = iota((slots, wide), 0) % FIELDS == iota((slots, wide), 1) // BLOCKS
        pick[...] = jnp.where(field, mm_nt(goes, reads), 0.0).astype(BF16)

    @pl.when(is_atmos)
    def _():
        entries = dst_ref.shape[1]
        square = (entries, entries)
        match = dst_ref[...] == me
        before = onehot(iota(square, 0) < iota(square, 1))
        rank = mm(onehot(match), before)
        block = (block_place(blk_ref[...]) + 1).astype(F32)
        slots = tiles * CAP * FIELDS
        spread = onehot(iota((tiles, slots), 1) // (CAP * FIELDS) == iota((tiles, slots), 0))
        which = (iota((SUB, slots), 1) // FIELDS) % CAP
        code = jnp.zeros((SUB, slots), F32)
        for r in range(CAP):
            value = jnp.where(match & (rank == r), block, 0.0).astype(BF16)
            row = mm_nt(jnp.ones((SUB, entries), BF16), value)
            code = jnp.where(which == r, mm(row.astype(BF16), spread), code)
        wide = FIELDS * BLOCKS
        shape = (wide, slots)
        lands = jnp.broadcast_to(code[:1], shape) == (iota(shape, 0) % BLOCKS + 1).astype(F32)
        field = iota(shape, 0) // BLOCKS == iota(shape, 1) % FIELDS
        place[...] = onehot(lands & field)

    def columns_packed():
        lane = iota((NY, CELLS), 1)
        rim = jnp.zeros((NY, CELLS), F32)
        for c in range(NC):
            rim = jnp.where(lane == c, pltpu.roll(vee[c, :, NX - CELLS :], c + 1, 1), rim)
            rim = jnp.where(lane == NC + c, pltpu.roll(vee[c, :, :CELLS], NC + c, 1), rim)
        return rim

    def halo_copies(i):
        def copy(j, source, target, y, x):
            return pltpu.make_async_remote_copy(
                src_ref=source, dst_ref=target, send_sem=halo_send.at[i, j], recv_sem=halo_recv.at[i, j],
                device_id=(sect, y, x), device_id_type=MESH,
            )

        return (
            copy(0, col_out.at[i], col_in.at[i, 0], gy, east),
            copy(1, col_out.at[i], col_in.at[i, 1], gy, west),
            copy(2, row_out.at[i, 1], row_in.at[i, 0], gy + 1, gx),
            copy(3, row_out.at[i, 0], row_in.at[i, 1], gy - 1, gx),
        )

    def prepare():
        for b in range(BANDS):
            rows = slice(b * SUB, (b + 1) * SUB)
            u = state[:, rows, :] * wet_f(rows)
            vee[:, rows, :] = u * dif[rows, :][None]
            u_hi[b], u_lo[b] = split(u.reshape(NC * SUB, NX))

    def wet_f(rows):
        return jnp.where(is_ocean, wet[rows, :].astype(F32), 1.0)[None]

    def rim_out(i):
        col_out[i] = columns_packed()
        for c in range(NC):
            row_out[i, 0, c : c + 1, :] = vee[c, :1, :]
            row_out[i, 1, c : c + 1, :] = vee[c, NY - 1 :, :]

    def rim_send(i):
        e, w, s, n = halo_copies(i)
        e.start()
        w.start()

        @pl.when(has_south)
        def _():
            s.start()

        @pl.when(has_north)
        def _():
            n.start()

    def rim_wait(i):
        e, w, s, n = halo_copies(i)
        e.wait()
        w.wait()

        @pl.when(has_south)
        def _():
            s.wait_send()
            n.wait_recv()

        @pl.when(has_north)
        def _():
            n.wait_send()
            s.wait_recv()

    def forced(coefs, fields):
        hi, lo = split(fields.reshape(FIELDS * SUB, NX))
        return mm(coefs[...], jnp.concatenate([hi, lo, hi], axis=0))

    def mix(k):
        for b in range(BANDS):
            rows = slice(b * SUB, (b + 1) * SUB)
            total = mm(k_hi[...], u_hi[b]) + mm(k_hi[...], u_lo[b]) + mm(k_lo[...], u_hi[b])
            total += forced(c_own, hist[k, :, rows, :])
            acc[:, rows, :] = total.reshape(NC, SUB, NX)

    def add_far(k, fields):
        for b in range(BANDS):
            rows = slice(b * SUB, (b + 1) * SUB)
            acc[:, rows, :] += forced(c_far, fields(rows)).reshape(NC, SUB, NX)

    def spread(i):
        row, lane = iota((NY, NX), 0), iota((NY, NX), 1)
        from_west, from_east = col_in[i, 0], col_in[i, 1]
        wet_all = jnp.where(is_ocean, wet[...].astype(F32), 1.0)
        for c in range(NC):
            v = vee[c]
            up = jnp.where(row == 0, jnp.broadcast_to(row_in[i, 0, c : c + 1, :], (NY, NX)), pltpu.roll(v, 1, 0))
            down = jnp.where(
                row == NY - 1, jnp.broadcast_to(row_in[i, 1, c : c + 1, :], (NY, NX)), pltpu.roll(v, NY - 1, 0)
            )
            left = jnp.where(
                lane == 0, jnp.broadcast_to(from_west[:, c : c + 1], (NY, NX)), pltpu.roll(v, 1, 1)
            )
            right = jnp.where(
                lane == NX - 1,
                jnp.broadcast_to(from_east[:, NC + c : NC + c + 1], (NY, NX)),
                pltpu.roll(v, NX - 1, 1),
            )
            state[c] = acc[c] + wet_all * state[c] + (((up + down) + (left + right)) - 4.0 * v)

    def deliver(k):
        surface = []
        for b in range(BANDS):
            surface.append(
                mm(e_hi[...], u_hi[b]) + mm(e_hi[...], u_lo[b]) + mm(e_lo[...], u_hi[b])
            )
        parts = [
            surface[b][q * SUB : (q + 1) * SUB, h * CELLS : (h + 1) * CELLS]
            for q in range(FIELDS) for h in range(2) for b in range(BANDS)
        ]
        hi, lo = split(jnp.concatenate(parts, axis=0))
        regridded = mm(hi, r_hi[...]) + mm(lo, r_hi[...]) + mm(hi, r_lo[...])
        hi, lo = split(regridded)
        slots = mm(pick[...], hi) + mm(pick[...], lo)
        packed[k] = slots.reshape(tiles, CAP * FIELDS, CELLS)

        def one(t, carry):
            y, x = lax.rem(gy + t // n_gx, n_gy), lax.rem(gx + t % n_gx, n_gx)
            pltpu.make_async_remote_copy(
                src_ref=packed.at[k, y * n_gx + x], dst_ref=arrived.at[k, me],
                send_sem=a2a_send.at[k], recv_sem=a2a_recv.at[k],
                device_id=(1, y, x), device_id_type=MESH,
            ).start()
            return carry

        lax.fori_loop(0, tiles, one, 0)

    def receive(k):
        pltpu.make_async_copy(arrived.at[k], arrived.at[k], a2a_recv.at[k]).wait()
        hi, lo = split(arrived[k].reshape(tiles * CAP * FIELDS, CELLS))
        sums = mm(place[...], hi) + mm(place[...], lo)
        for q in range(FIELDS):
            for h in range(2):
                start = (q * 2 + h) * NY
                far[k, q, :, h * CELLS : (h + 1) * CELLS] = sums[start : start + NY]
        for b in range(BANDS):
            rows = slice(b * SUB, (b + 1) * SUB)
            state[:, rows, :] += forced(c_far, far[k, :, rows, :]).reshape(NC, SUB, NX)

    def far_copy(k, target_sect):
        return pltpu.make_async_remote_copy(
            src_ref=his_hbm.at[0, k], dst_ref=far.at[k], send_sem=far_send.at[k], recv_sem=far_recv.at[k],
            device_id=(target_sect, gy, gx), device_id_type=MESH,
        )

    prepare()
    rim_out(0)

    peers = jnp.where(is_ocean, tiles, 1) + 2 + jnp.where(has_north, 1, 0) + jnp.where(has_south, 1, 0)
    pl.semaphore_wait(barrier, peers)
    rim_send(0)

    @pl.when(is_atmos)
    def _():
        for k in range(STEPS - 1, -1, -1):
            far_copy(k, 0).start()

    loads[-1].wait()

    def step(i, carry):
        k = STEPS - 1 - i
        mix(k)

        @pl.when(is_ocean)
        def _():
            far_copy(k, 1).wait_recv()
            add_far(k, lambda rows: far[k, :, rows, :])

        rim_wait(i)
        spread(i)

        @pl.when(is_atmos)
        def _():
            receive(k)

        @pl.when(i < STEPS - 1)
        def _():
            prepare()
            rim_out(i + 1)
            rim_send(i + 1)

        @pl.when(is_ocean)
        def _():
            @pl.when(i == STEPS - 1)
            def _():
                prepare()

            deliver(k)

        return carry

    lax.fori_loop(0, STEPS, step, 0)
    out = pltpu.make_async_copy(state, out_hbm.at[0], out_sem)
    out.start()

    @pl.when(is_ocean)
    def _():
        for k in range(STEPS):
            pltpu.make_async_copy(packed.at[k], packed.at[k], a2a_send.at[k]).wait()

    @pl.when(is_atmos)
    def _():
        for k in range(STEPS):
            far_copy(k, 0).wait_send()

    out.wait()


def body(n_gy, n_gx, adj, dif, mix, cou, his, ext, msk, reg, dst, src, blk):
    tiles = n_gy * n_gx
    entries = src.shape[0] // tiles
    tables = [x.reshape(tiles, entries) for x in (dst, src, blk)]
    anywhere = pl.BlockSpec(memory_space=pl.ANY)
    rows, slots, wide = NC * SUB, tiles * CAP * FIELDS, FIELDS * BLOCKS
    dma = pltpu.SemaphoreType.DMA
    return pl.pallas_call(
        functools.partial(kernel, n_gy, n_gx),
        out_shape=jax.ShapeDtypeStruct(adj.shape, F32),
        in_specs=[anywhere] * 11,
        out_specs=anywhere,
        scratch_shapes=[
            pltpu.VMEM((NC, NC), F32),
            pltpu.VMEM((2 * FIELDS, NC), F32),
            pltpu.VMEM((FIELDS, NC), F32),
            pltpu.VMEM((CELLS, CELLS), F32),
            pltpu.VMEM((tiles, entries), jnp.int32),
            pltpu.VMEM((tiles, entries), jnp.int32),
            pltpu.VMEM((tiles, entries), jnp.int32),
            pltpu.VMEM((NC, NY, NX), F32),
            pltpu.VMEM((NY, NX), jnp.int32),
            pltpu.VMEM((NY, NX), F32),
            pltpu.VMEM((STEPS, FIELDS, NY, NX), F32),
            pltpu.VMEM((STEPS, FIELDS, NY, NX), F32),
            pltpu.VMEM((NC, NY, NX), F32),
            pltpu.VMEM((NC, NY, NX), F32),
            pltpu.VMEM((BANDS, rows, NX), BF16),
            pltpu.VMEM((BANDS, rows, NX), BF16),
            pltpu.VMEM((rows, rows), BF16),
            pltpu.VMEM((rows, rows), BF16),
            pltpu.VMEM((rows, 3 * FIELDS * SUB), BF16),
            pltpu.VMEM((rows, 3 * FIELDS * SUB), BF16),
            pltpu.VMEM((FIELDS * SUB, rows), BF16),
            pltpu.VMEM((FIELDS * SUB, rows), BF16),
            pltpu.VMEM((CELLS, CELLS), BF16),
            pltpu.VMEM((CELLS, CELLS), BF16),
            pltpu.VMEM((slots, wide), BF16),
            pltpu.VMEM((wide, slots), BF16),
            pltpu.VMEM((STEPS, tiles, CAP * FIELDS, CELLS), F32),
            pltpu.VMEM((STEPS, tiles, CAP * FIELDS, CELLS), F32),
            pltpu.VMEM((STEPS, 2, NC, NX), F32),
            pltpu.VMEM((STEPS, 2, NC, NX), F32),
            pltpu.VMEM((STEPS, NY, CELLS), F32),
            pltpu.VMEM((STEPS, 2, NY, CELLS), F32),
            dma((11,)), dma((STEPS,)), dma((STEPS,)), dma((STEPS, 4)), dma((STEPS, 4)),
            dma((STEPS,)), dma((STEPS,)), dma,
        ],
        compiler_params=pltpu.CompilerParams(
            collective_id=0, has_side_effects=True, vmem_limit_bytes=67043328
        ),
    )(adj, dif, mix, cou.swapaxes(1, 2), his, ext, msk, reg, *tables)


def solution(mesh):
    placed = (
        P("sect", None, "gy", "gx"), P("sect", "gy", "gx"), P("sect", None, None), P("sect", None, None),
        P("sect", None, None, "gy", "gx"), P(), P("gy", "gx"), P(("gy", "gx"), None, None), P(), P(), P(),
    )
    return jax.shard_map(
        functools.partial(body, mesh.shape["gy"], mesh.shape["gx"]),
        mesh=mesh, in_specs=placed, out_specs=P("sect", None, "gy", "gx"), check_vma=False,
    )
```

profile of v0, /device:TPU:1, one launch (start us, length us, event | category | flops | bytes accessed | tf_op | source)
XLA Modules:
  0.0 53.7 jit_solution(915660980172305526)
XLA Ops:
  0.0 51.4 %shard_map.109 = f32[1,32,32,256]{3,2,1,0:T(8,128)} custom-call(f32[1,32,32,256]{3,2,1,0:T(8,128)} %adj_hbm.1, f32[1,32,256]{2,1,0:T(8,128)} %dif_hbm.1, f32[1,32,32]{2,1,0:T(8,128)} %mix_hbm.1, f32[1,8,32]{2,1,0:T(8,128)} %bitcast.7, f32[1,4,4,32,256]{4,3,2,1,0:T(8,128)} %his_hbm.1, f32[4,32]{1,0:T(4,128)} %ext_hbm.1, s32[32,256]{1,0:T(8,128)} %msk_hbm.1, ...), custom_call_target="tpu_custom_call" | custom-call | tf_op jit(solution)/shard_map/pallas_call | solution.py:390
  51.4 2.3 %copy.13 = f32[1,32,32,256]{3,2,1,0:T(8,128)} copy(f32[1,32,32,256]{3,2,1,0:T(8,128)} %shard_map.109) | data formatting | bytes 2097152
where the time goes:
time: 53.8 us; the launch traced here: 53.7 us
  Pallas kernels  51.4 us (96%)
  local copies, waits for them, and re-layouts  2.31 us (4%)
    pallas_call x1, Pallas kernels, body(): pl.pallas_call(functools.partial(kernel, n_gy, n_gx), out_shape=jax.Shape...  51.4 us
    unnamed x1, local copies, waits for them, and re-layouts  2.31 us

commit v1 on v0

v1 whole, which is shorter than its diff:
```python
import functools
import itertools
import math

import jax
import jax.numpy as jnp
from jax import lax
from jax.experimental import pallas as pl
from jax.experimental.pallas import tpu as pltpu
from jax.sharding import PartitionSpec as P

MESH = pl.DeviceIdType.MESH
F32, BF16 = jnp.float32, jnp.bfloat16
NC, NY, NX = 32, 32, 256
STEPS, FIELDS = 4, 4
SUB = 8
BANDS = NY // SUB
CELLS = 128
BLOCKS = NY * NX // CELLS
CAP = 2
NT = (((1,), (1,)), ((), ()))


def iota(shape, axis):
    return lax.broadcasted_iota(jnp.int32, shape, axis)


def split(x):
    hi = x.astype(BF16)
    return hi, (x - hi.astype(F32)).astype(BF16)


def mm(a, b):
    return jnp.dot(a, b, preferred_element_type=F32)


def mm_nt(a, b):
    return lax.dot_general(a, b, NT, preferred_element_type=F32)


def onehot(cond):
    return jnp.where(cond, 1.0, 0.0).astype(BF16)


def widen(small):
    rows, columns = small.shape
    left = onehot(iota((rows * SUB, rows), 0) // SUB == iota((rows * SUB, rows), 1))
    right = onehot(iota((columns, columns * SUB), 1) // SUB == iota((columns, columns * SUB), 0))
    big = (rows * SUB, columns * SUB)
    same = iota(big, 0) % SUB == iota(big, 1) % SUB
    return [
        jnp.where(same, mm(mm(left, part).astype(BF16), right), 0.0).astype(BF16)
        for part in split(small)
    ]


def block_place(block):
    return (block % 2) * NY + block // 2


def kernel(
    n_gy, n_gx,
    adj_hbm, dif_hbm, mix_hbm, cou_hbm, his_hbm, ext_hbm, msk_hbm, reg_hbm, dst_hbm, src_hbm, blk_hbm,
    out_ref,
    mix_ref, cou_ref, ext_ref, reg_ref, dst_ref, src_ref, blk_ref,
    wet, dif, hist, far, vee, acc, u_hi, u_lo, k_hi, k_lo, c_own, c_far, e_hi, e_lo, r_hi, r_lo,
    pick, place, packed, arrived, row_out, row_in, col_out, col_in,
    late, late_vee, late_row_out, late_row_in, late_col_out, late_col_in,
    load_sem, ready, far_send, far_recv, halo_send, halo_recv, a2a_send, a2a_recv, late_send, late_recv,
):
    sect, gy, gx = lax.axis_index("sect"), lax.axis_index("gy"), lax.axis_index("gx")
    tiles = n_gy * n_gx
    me = gy * n_gx + gx
    is_ocean, is_atmos = sect == 0, sect == 1
    west, east = lax.rem(gx + n_gx - 1, n_gx), lax.rem(gx + 1, n_gx)
    side = math.isqrt(n_gy)

    def farthest_first():
        def hops(offset):
            return sum(min(d, n - d) for d, n in zip(offset, (side, side, n_gx)))

        along_x = [lax.rem(gy // side + t, side) * side for t in range(side)]
        along_y = [lax.rem(lax.rem(gy, side) + t, side) for t in range(side)]
        along_z = [lax.rem(gx + t, n_gx) for t in range(n_gx)]
        offsets = itertools.product(range(side), range(side), range(n_gx))
        return [(along_x[i] + along_y[j], along_z[l]) for i, j, l in sorted(offsets, key=hops, reverse=True)]

    has_north, has_south = gy > 0, gy < n_gy - 1
    barrier = pltpu.get_barrier_semaphore()
    state = out_ref.at[0]

    loads = [
        pltpu.make_async_copy(source, target, load_sem.at[j])
        for j, (source, target) in enumerate(
            (
                (adj_hbm.at[0], state), (dif_hbm.at[0], dif), (msk_hbm, wet), (mix_hbm.at[0], mix_ref),
                (cou_hbm.at[0], cou_ref), (ext_hbm, ext_ref), (dst_hbm, dst_ref), (src_hbm, src_ref),
                (blk_hbm, blk_ref), (reg_hbm.at[0], reg_ref), (his_hbm.at[0], hist),
            )
        )
    ]
    for load in loads:
        load.start()

    def signal(s, y, x):
        pl.semaphore_signal(barrier, inc=1, device_id=(s, y, x), device_id_type=MESH)

    @pl.when(gy == 0)
    def _():
        for ref in (row_in, late_row_in):
            ref[:, 0] = jnp.zeros_like(ref[:, 0])

    @pl.when(gy == n_gy - 1)
    def _():
        for ref in (row_in, late_row_in):
            ref[:, 1] = jnp.zeros_like(ref[:, 1])

    signal(sect, gy, west)
    signal(sect, gy, east)

    @pl.when(is_ocean)
    def _():
        for t in range(1, n_gy):
            signal(0, lax.rem(gy + t, n_gy), gx)
        signal(1, gy, gx)

    @pl.when(is_atmos)
    def _():
        for t in range(n_gx):
            signal(0, gy, lax.rem(gx + t, n_gx))

        @pl.when(has_north)
        def _():
            signal(1, gy - 1, gx)

        @pl.when(has_south)
        def _():
            signal(1, gy + 1, gx)

    def halo_copies(i):
        return rim_copies(i, col_out, col_in, row_out, row_in, halo_send, halo_recv)

    def rim_copies(i, col_out, col_in, row_out, row_in, halo_send, halo_recv):
        def copy(j, source, target, y, x):
            return pltpu.make_async_remote_copy(
                src_ref=source, dst_ref=target, send_sem=halo_send.at[i, j], recv_sem=halo_recv.at[i, j],
                device_id=(sect, y, x), device_id_type=MESH,
            )

        return (
            copy(0, col_out.at[i, 0], col_in.at[i, 0], gy, east),
            copy(1, col_out.at[i, 1], col_in.at[i, 1], gy, west),
            copy(2, row_out.at[i, 1], row_in.at[i, 0], gy + 1, gx),
            copy(3, row_out.at[i, 0], row_in.at[i, 1], gy - 1, gx),
        )

    def prepare():
        for b in range(BANDS):
            rows = slice(b * SUB, (b + 1) * SUB)
            u = state[:, rows, :] * wet_f(rows)
            vee[:, rows, :] = u * dif[rows, :][None]
            u_hi[b], u_lo[b] = split(u.reshape(NC * SUB, NX))

    def wet_f(rows):
        return jnp.where(is_ocean, wet[rows, :].astype(F32), 1.0)[None]

    def rim_out(i):
        rim_pack(i, vee, NC, col_out, row_out)

    def rim_pack(i, vee, count, col_out, row_out):
        lane = iota((SUB, CELLS), 1)
        east_rim, west_rim = jnp.zeros((SUB, CELLS), F32), jnp.zeros((SUB, CELLS), F32)
        for c in range(count):
            row_out[i, 0, c : c + 1, :] = vee[c, :1, :]
            row_out[i, 1, c : c + 1, :] = vee[c, NY - 1 :, :]
            for b in range(BANDS):
                rows, at = slice(b * SUB, (b + 1) * SUB), b * NC + c
                east_rim = jnp.where(
                    lane == at, pltpu.roll(vee[c, rows, NX - CELLS :], (at + 1) % CELLS, 1), east_rim
                )
                west_rim = jnp.where(lane == at, pltpu.roll(vee[c, rows, :CELLS], at, 1) if at else vee[c, rows, :CELLS], west_rim)
        col_out[i, 0], col_out[i, 1] = east_rim, west_rim

    def rim_send(i, copies=halo_copies):
        e, w, s, n = copies(i)
        e.start()
        w.start()

        @pl.when(has_south)
        def _():
            s.start()

        @pl.when(has_north)
        def _():
            n.start()

    def rim_wait(i, copies=halo_copies):
        e, w, s, n = copies(i)
        e.wait()
        w.wait()

        @pl.when(has_south)
        def _():
            s.wait_send()
            n.wait_recv()

        @pl.when(has_north)
        def _():
            n.wait_send()
            s.wait_recv()

    def forced(coefs, fields):
        hi, lo = split(fields.reshape(FIELDS * SUB, NX))
        return mm(coefs, jnp.concatenate([hi, lo, hi], axis=0))

    def mix(k):
        for b in range(BANDS):
            rows = slice(b * SUB, (b + 1) * SUB)
            total = mm(k_hi[...], u_hi[b]) + mm(k_hi[...], u_lo[b]) + mm(k_lo[...], u_hi[b])
            total += forced(c_own[...], hist[k, :, rows, :])
            acc[:, rows, :] = total.reshape(NC, SUB, NX)

    def add_far(target, j, fields):
        for b in range(BANDS):
            rows = slice(b * SUB, (b + 1) * SUB)
            target[:, rows, :] += forced(c_far[j], fields[:, rows, :]).reshape(NC, SUB, NX)

    def laplace(i, c, vee, col_in, row_in):
        row, lane = iota((NY, NX), 0), iota((NY, NX), 1)
        v = vee[c]
        north, south = row_in[i, 0, c : c + 1, :], row_in[i, 1, c : c + 1, :]
        whole = (NY, NX)

        def column(j):
            bands = [col_in[i, j, :, b * NC + c : b * NC + c + 1] for b in range(BANDS)]
            return jnp.concatenate([jnp.broadcast_to(x, (SUB, CELLS)) for x in bands], axis=0)

        from_west, from_east = column(0), column(1)
        up = jnp.where(row == 0, jnp.broadcast_to(north, whole), pltpu.roll(v, 1, 0))
        down = jnp.where(row == NY - 1, jnp.broadcast_to(south, whole), pltpu.roll(v, NY - 1, 0))
        left = jnp.where(lane == 0, jnp.concatenate([from_west] * 2, axis=1), pltpu.roll(v, 1, 1))
        right = jnp.where(lane == NX - 1, jnp.concatenate([from_east] * 2, axis=1), pltpu.roll(v, NX - 1, 1))
        return ((up + down) + (left + right)) - 4.0 * v

    def spread(i):
        wet_all = jnp.where(is_ocean, wet[...].astype(F32), 1.0)
        for c in range(NC):
            state[c] = acc[c] + wet_all * state[c] + laplace(i, c, vee, col_in, row_in)

    def deliver(k):
        surface = []
        for b in range(BANDS):
            surface.append(
                mm(e_hi[...], u_hi[b]) + mm(e_hi[...], u_lo[b]) + mm(e_lo[...], u_hi[b])
            )
        parts = [
            surface[b][q * SUB : (q + 1) * SUB, h * CELLS : (h + 1) * CELLS]
            for q in range(FIELDS) for h in range(2) for b in range(BANDS)
        ]
        hi, lo = split(jnp.concatenate(parts, axis=0))
        regridded = mm(hi, r_hi[...]) + mm(lo, r_hi[...]) + mm(hi, r_lo[...])
        hi, lo = split(regridded)
        slots = mm(pick[...], hi) + mm(pick[...], lo)
        packed[k] = slots.reshape(tiles, CAP * FIELDS, CELLS)

        for y, x in farthest_first():
            pltpu.make_async_remote_copy(
                src_ref=packed.at[k, y * n_gx + x], dst_ref=arrived.at[k, me],
                send_sem=a2a_send.at[k], recv_sem=a2a_recv.at[k],
                device_id=(1, y, x), device_id_type=MESH,
            ).start()

    def receive(k):
        pltpu.make_async_copy(arrived.at[k], arrived.at[k], a2a_recv.at[k]).wait()
        hi, lo = split(arrived[k].reshape(tiles * CAP * FIELDS, CELLS))
        sums = mm(place[...], hi) + mm(place[...], lo)
        for q in range(FIELDS):
            for h in range(2):
                start = (q * 2 + h) * NY
                far[k, q, :, h * CELLS : (h + 1) * CELLS] = sums[start : start + NY]

    def late_copies(n):
        return rim_copies(n, late_col_out, late_col_in, late_row_out, late_row_in, late_send, late_recv)

    def late_start(n, fields):
        for j, field in enumerate(fields):
            for q in range(FIELDS):
                late_vee[j * FIELDS + q] = field[q] * dif[...]
        rim_pack(n, late_vee, len(fields) * FIELDS, late_col_out, late_row_out)
        rim_send(n, late_copies)

    def late_end(n, outputs):
        rim_wait(n, late_copies)
        for j, (ref, q_of) in enumerate(outputs):
            for q in range(FIELDS):
                ref[q] = q_of(laplace(n, j * FIELDS + q, late_vee, late_col_in, late_row_in), q)

    def atmosphere_end():
        first, second = late.at[0], late.at[1]
        receive(3)
        late_start(0, [far.at[3]])
        add_far(state, 3, far.at[3])
        late_end(0, [(first, lambda x, q: x)])
        receive(2)
        for q in range(FIELDS):
            x, r = first[q], far[2, q]
            first[q] = x + r
            second[q] = 3.0 * x + 2.0 * r
            far[3, q] = 3.0 * x + r
        late_start(1, [first, second])
        add_far(state, 2, far.at[3])
        late_end(1, [(first, lambda x, q: x), (second, lambda x, q: x)])
        receive(1)
        for q in range(FIELDS):
            r = far[1, q]
            first[q] += r
            second[q] += r
        late_start(2, [first])
        add_far(state, 1, second)
        late_end(2, [(first, lambda x, q: x)])
        receive(0)
        for q in range(FIELDS):
            first[q] += far[0, q]
        add_far(state, 0, first)

    def far_copy(k, target_sect):
        return pltpu.make_async_remote_copy(
            src_ref=his_hbm.at[0, k], dst_ref=far.at[k], send_sem=far_send.at[k], recv_sem=far_recv.at[k],
            device_id=(target_sect, gy, gx), device_id_type=MESH,
        )

    for load in loads[:3]:
        load.wait()
    prepare()
    rim_out(0)

    beside = jnp.where(has_north, 1, 0) + jnp.where(has_south, 1, 0)
    pl.semaphore_wait(barrier, 2 + jnp.where(is_ocean, n_gx + n_gy - 1, 1 + beside))
    rim_send(0)

    @pl.when(is_ocean)
    def _():
        for t in range(1, n_gy):
            pl.semaphore_signal(
                ready, inc=1, device_id=(0, lax.rem(gy + t, n_gy), gx), device_id_type=MESH
            )

    @pl.when(is_atmos)
    def _():
        for k in range(STEPS - 1, -1, -1):
            far_copy(k, 0).start()

    for load in loads[3:]:
        load.wait()

    k_hi[...], k_lo[...] = widen(mix_ref[...].T)

    def triple(small):
        hi, lo = widen(small)
        return jnp.concatenate([hi, hi, lo], axis=1)

    c_own[...] = triple(cou_ref[:FIELDS, :].T)
    c_far[0] = triple(cou_ref[FIELDS:, :].T)

    @pl.when(is_ocean)
    def _():
        e_hi[...], e_lo[...] = widen(ext_ref[...])
        r_hi[...], r_lo[...] = split(reg_ref[...])
        entries = dst_ref.shape[1]
        dest = dst_ref[pl.ds(me, 1), :]
        source = block_place(src_ref[pl.ds(me, 1), :])
        dest_row = jnp.broadcast_to(dest, (entries, entries))
        dest_col = dest_row.T
        square = (entries, entries)
        earlier = (dest_row == dest_col) & (iota(square, 0) < iota(square, 1))
        rank = jnp.sum(jnp.where(earlier, 1, 0), axis=0, keepdims=True)
        position = dest * CAP + rank
        slots = tiles * CAP * FIELDS
        goes = onehot(jnp.broadcast_to(position, (slots, entries)) == iota((slots, entries), 0) // FIELDS)
        wide = FIELDS * BLOCKS
        reads = onehot(jnp.broadcast_to(source, (wide, entries)) == iota((wide, entries), 0) % BLOCKS)
        field = iota((slots, wide), 0) % FIELDS == iota((slots, wide), 1) // BLOCKS
        pick[...] = jnp.where(field, mm_nt(goes, reads), 0.0).astype(BF16)

    @pl.when(is_atmos)
    def _():
        entries = dst_ref.shape[1]
        square = (entries, entries)
        match = dst_ref[...] == me
        before = onehot(iota(square, 0) < iota(square, 1))
        rank = mm(onehot(match), before)
        block = (block_place(blk_ref[...]) + 1).astype(F32)
        slots = tiles * CAP * FIELDS
        spread = onehot(iota((tiles, slots), 1) // (CAP * FIELDS) == iota((tiles, slots), 0))
        which = (iota((SUB, slots), 1) // FIELDS) % CAP
        code = jnp.zeros((SUB, slots), F32)
        for r in range(CAP):
            value = jnp.where(match & (rank == r), block, 0.0).astype(BF16)
            row = mm_nt(jnp.ones((SUB, entries), BF16), value)
            code = jnp.where(which == r, mm(row.astype(BF16), spread), code)
        wide = FIELDS * BLOCKS
        shape = (wide, slots)
        lands = jnp.broadcast_to(code[:1], shape) == (iota(shape, 0) % BLOCKS + 1).astype(F32)
        field = iota(shape, 0) // BLOCKS == iota(shape, 1) % FIELDS
        place[...] = onehot(lands & field)
        mixed = cou_ref[FIELDS:, :].T
        for j in range(1, STEPS):
            mixed += jnp.dot(
                mix_ref[...].T, mixed, precision=lax.Precision.HIGHEST, preferred_element_type=F32
            )
            c_far[j] = triple(mixed)

    def step(i, carry):
        k = STEPS - 1 - i
        mix(k)

        @pl.when(is_ocean)
        def _():
            far_copy(k, 1).wait_recv()
            add_far(acc, 0, far.at[k])

        rim_wait(i)
        spread(i)

        @pl.when(i < STEPS - 1)
        def _():
            prepare()
            rim_out(i + 1)
            rim_send(i + 1)

        @pl.when(is_ocean)
        def _():
            @pl.when(i == STEPS - 1)
            def _():
                prepare()

            @pl.when(i == 0)
            def _():
                pl.semaphore_wait(ready, n_gy - 1)

            deliver(k)

        return carry

    lax.fori_loop(0, STEPS, step, 0)

    @pl.when(is_atmos)
    def _():
        atmosphere_end()

    @pl.when(is_ocean)
    def _():
        for k in range(STEPS):
            pltpu.make_async_copy(packed.at[k], packed.at[k], a2a_send.at[k]).wait()

    @pl.when(is_atmos)
    def _():
        for k in range(STEPS):
            far_copy(k, 0).wait_send()


def body(n_gy, n_gx, adj, dif, mix, cou, his, ext, msk, reg, dst, src, blk):
    tiles = n_gy * n_gx
    entries = src.shape[0] // tiles
    tables = [x.reshape(tiles, entries) for x in (dst, src, blk)]
    anywhere = pl.BlockSpec(memory_space=pl.ANY)
    rows, slots, wide = NC * SUB, tiles * CAP * FIELDS, FIELDS * BLOCKS
    dma = pltpu.SemaphoreType.DMA
    return pl.pallas_call(
        functools.partial(kernel, n_gy, n_gx),
        out_shape=pltpu.VMEM(adj.shape, F32),
        in_specs=[anywhere] * 11,
        out_specs=pl.BlockSpec(memory_space=pltpu.VMEM),
        scratch_shapes=[
            pltpu.VMEM((NC, NC), F32),
            pltpu.VMEM((2 * FIELDS, NC), F32),
            pltpu.VMEM((FIELDS, NC), F32),
            pltpu.VMEM((CELLS, CELLS), F32),
            pltpu.VMEM((tiles, entries), jnp.int32),
            pltpu.VMEM((tiles, entries), jnp.int32),
            pltpu.VMEM((tiles, entries), jnp.int32),
            pltpu.VMEM((NY, NX), jnp.int32),
            pltpu.VMEM((NY, NX), F32),
            pltpu.VMEM((STEPS, FIELDS, NY, NX), F32),
            pltpu.VMEM((STEPS, FIELDS, NY, NX), F32),
            pltpu.VMEM((NC, NY, NX), F32),
            pltpu.VMEM((NC, NY, NX), F32),
            pltpu.VMEM((BANDS, rows, NX), BF16),
            pltpu.VMEM((BANDS, rows, NX), BF16),
            pltpu.VMEM((rows, rows), BF16),
            pltpu.VMEM((rows, rows), BF16),
            pltpu.VMEM((rows, 3 * FIELDS * SUB), BF16),
            pltpu.VMEM((STEPS, rows, 3 * FIELDS * SUB), BF16),
            pltpu.VMEM((FIELDS * SUB, rows), BF16),
            pltpu.VMEM((FIELDS * SUB, rows), BF16),
            pltpu.VMEM((CELLS, CELLS), BF16),
            pltpu.VMEM((CELLS, CELLS), BF16),
            pltpu.VMEM((slots, wide), BF16),
            pltpu.VMEM((wide, slots), BF16),
            pltpu.VMEM((STEPS, tiles, CAP * FIELDS, CELLS), F32),
            pltpu.VMEM((STEPS, tiles, CAP * FIELDS, CELLS), F32),
            pltpu.VMEM((STEPS, 2, NC, NX), F32),
            pltpu.VMEM((STEPS, 2, NC, NX), F32),
            pltpu.VMEM((STEPS, 2, SUB, CELLS), F32),
            pltpu.VMEM((STEPS, 2, SUB, CELLS), F32),
            pltpu.VMEM((2, FIELDS, NY, NX), F32),
            pltpu.VMEM((2 * FIELDS, NY, NX), F32),
            pltpu.VMEM((STEPS - 1, 2, 2 * FIELDS, NX), F32),
            pltpu.VMEM((STEPS - 1, 2, 2 * FIELDS, NX), F32),
            pltpu.VMEM((STEPS - 1, 2, SUB, CELLS), F32),
            pltpu.VMEM((STEPS - 1, 2, SUB, CELLS), F32),
            dma((11,)), pltpu.SemaphoreType.REGULAR, dma((STEPS,)), dma((STEPS,)), dma((STEPS, 4)), dma((STEPS, 4)),
            dma((STEPS,)), dma((STEPS,)), dma((STEPS - 1, 4)), dma((STEPS - 1, 4)),
        ],
        compiler_params=pltpu.CompilerParams(
            collective_id=0, has_side_effects=True, vmem_limit_bytes=60 * 1024 * 1024
        ),
    )(adj, dif, mix, cou.swapaxes(1, 2), his, ext, msk, reg, *tables)


def solution(mesh):
    placed = (
        P("sect", None, "gy", "gx"), P("sect", "gy", "gx"), P("sect", None, None), P("sect", None, None),
        P("sect", None, None, "gy", "gx"), P(), P("gy", "gx"), P(("gy", "gx"), None, None), P(), P(), P(),
    )
    return jax.shard_map(
        functools.partial(body, mesh.shape["gy"], mesh.shape["gx"]),
        mesh=mesh, in_specs=placed, out_specs=P("sect", None, "gy", "gx"), check_vma=False,
    )
```

time: 53.8 us -> 46.9 us (0.87)
  Pallas kernels: 51.4 us -> 45.8 us
  local copies, waits for them, and re-layouts: 2.31 us -> 0.97 us
    pallas_call x1, Pallas kernels: 51.4 us -> 45.8 us  [body(): pl.pallas_call(functools.partial(kernel, n_gy, n_gx), out_shape=pltpu.VME...]
    unnamed x1, local copies, waits for them, and re-layouts: 2.31 us -> 0.97 us
where the time goes in v1:
time: 46.9 us; the launch traced here: 46.8 us
  Pallas kernels  45.8 us (98%)
  local copies, waits for them, and re-layouts  0.97 us (2%)
    pallas_call x1, Pallas kernels, body(): pl.pallas_call(functools.partial(kernel, n_gy, n_gx), out_shape=pltpu.VME...  45.8 us
    unnamed x1, local copies, waits for them, and re-layouts  0.97 us

profile of v1, /device:TPU:1, one launch (start us, length us, event | category | flops | bytes accessed | tf_op | source)
XLA Modules:
  0.0 46.8 jit_solution(3603529588072553479)
XLA Ops:
  0.0 45.8 %shard_map.109 = f32[1,32,32,256]{3,2,1,0:T(8,128)S(1)} custom-call(f32[1,32,32,256]{3,2,1,0:T(8,128)} %adj_hbm.1, f32[1,32,256]{2,1,0:T(8,128)} %dif_hbm.1, f32[1,32,32]{2,1,0:T(8,128)} %mix_hbm.1, f32[1,8,32]{2,1,0:T(8,128)} %bitcast.7, f32[1,4,4,32,256]{4,3,2,1,0:T(8,128)} %his_hbm.1, f32[4,32]{1,0:T(4,128)} %ext_hbm.1, s32[32,256]{1,0:T(8,128)} %msk_hbm.1, ...), custom_call_target="tpu_custom_call" | custom-call | tf_op jit(solution)/shard_map/pallas_call | solution.py:469
  45.8 1.0 %copy.13 = f32[1,32,32,256]{3,2,1,0:T(8,128)} copy(f32[1,32,32,256]{3,2,1,0:T(8,128)S(1)} %shard_map.109) | data formatting | bytes 2097152

commit v2 on v1

--- a/solution.py
+++ b/solution.py
@@ -99,8 +99,6 @@
             )
         )
     ]
-    for load in loads:
-        load.start()
 
     def signal(s, y, x):
         pl.semaphore_signal(barrier, inc=1, device_id=(s, y, x), device_id_type=MESH)
@@ -136,6 +134,9 @@
         @pl.when(has_south)
         def _():
             signal(1, gy + 1, gx)
+
+    for load in loads:
+        load.start()
 
     def halo_copies(i):
         return rim_copies(i, col_out, col_in, row_out, row_in, halo_send, halo_recv)
@@ -183,16 +184,17 @@
 
     def rim_send(i, copies=halo_copies):
         e, w, s, n = copies(i)
+
+        @pl.when(has_south)
+        def _():
+            s.start()
+
+        @pl.when(has_north)
+        def _():
+            n.start()
+
         e.start()
         w.start()
-
-        @pl.when(has_south)
-        def _():
-            s.start()
-
-        @pl.when(has_north)
-        def _():
-            n.start()
 
     def rim_wait(i, copies=halo_copies):
         e, w, s, n = copies(i)

time: 46.9 us -> 46.7 us (level)
  no operation moved by 1% of the time
where the time goes in v2:
time: 46.7 us; the launch traced here: 46.6 us
  Pallas kernels  45.6 us (98%)
  local copies, waits for them, and re-layouts  0.97 us (2%)
    pallas_call x1, Pallas kernels, body(): pl.pallas_call(functools.partial(kernel, n_gy, n_gx), out_shape=pltpu.VME...  45.6 us
    unnamed x1, local copies, waits for them, and re-layouts  0.97 us

profile of v2, /device:TPU:1, one launch (start us, length us, event | category | flops | bytes accessed | tf_op | source)
XLA Modules:
  0.0 46.6 jit_solution(18227790147281659499)
XLA Ops:
  0.0 45.6 %shard_map.109 = f32[1,32,32,256]{3,2,1,0:T(8,128)S(1)} custom-call(f32[1,32,32,256]{3,2,1,0:T(8,128)} %adj_hbm.1, f32[1,32,256]{2,1,0:T(8,128)} %dif_hbm.1, f32[1,32,32]{2,1,0:T(8,128)} %mix_hbm.1, f32[1,8,32]{2,1,0:T(8,128)} %bitcast.7, f32[1,4,4,32,256]{4,3,2,1,0:T(8,128)} %his_hbm.1, f32[4,32]{1,0:T(4,128)} %ext_hbm.1, s32[32,256]{1,0:T(8,128)} %msk_hbm.1, ...), custom_call_target="tpu_custom_call" | custom-call | tf_op jit(solution)/shard_map/pallas_call | solution.py:471
  45.6 1.0 %copy.13 = f32[1,32,32,256]{3,2,1,0:T(8,128)} copy(f32[1,32,32,256]{3,2,1,0:T(8,128)S(1)} %shard_map.109) | data formatting | bytes 2097152
